TPU v7x, 32 devices: a whole 2x2x4 slice. The times are simulated.
32 devices in a mesh: area: 8 (over y, x, core), layer: 4 (over z).
Axes of the slice: x: 2, y: 2, z: 4, core: 2. Of those that a mesh axis runs over, the one named last changes fastest.
Arguments:
- permeability: float32 [16, 4096, 512], P('layer', 'area'), may hold values from 0.1 to 10
- mobility: float32 [16, 4096, 512], P('layer', 'area'), may hold values from 0.3 to 3
- thickness: float32 [16], P('layer'), may hold values from 0.5 to 2
- caprock: int32 [4096, 512], P('area'), may hold values from 0 to 7
- plume: int32 [4096, 512], P('area'), may hold values from 0 to 15
- storage: float32 [4096, 512], P('area'), may hold values from 1.6 to 16
- source: float32 [4096, 512], P('area'), may hold values from -192 to 192
- pressure_old: float32 [4096, 512], P('area'), may hold values from -6 to 6
Outputs:
- cell_pressure: float32 [16, 4096, 512], P('layer', 'area')
- flux_rows: float32 [16, 4096, 512], P('layer', 'area')
- flux_cols: float32 [16, 4096, 512], P('layer', 'area')
Inputs may be any that keep to these rules, and one draw needn't show every extreme that they name: Layers above layer caprock of a column are sealed rock. CO2 fills the open layers above layer plume of a column; where plume <= caprock a column holds no CO2.
All inputs are finite; a program needn't handle non-finite values.
Results may differ from a plain program's by a relative error of at most 0.0003.
Values sent between devices are 32-bit elements; how exact they have to be, the bound alone decides.
No kernel may reach another device: no remote copies, remote signals or barrier semaphores. Data moves between devices by JAX's collectives and lax.ppermute only.
A program may use at most 128 MiB of HBM per device.

v0:
```python
import jax
import jax.numpy as jnp
from jax import lax
from jax.sharding import PartitionSpec as P

SWEEPS = 3
buoyancy_scale = 0.3
gravity_scale = 0.05
gas_density = 0.7
brine_density = 1.0


def padded_2(block, sides, width):
    for axis, dim in sides:
        count = lax.axis_size(axis)
        forward = [(i, i + 1) for i in range(count - 1)]
        backward = [(target, source) for source, target in forward]
        low = lax.ppermute(
            lax.slice_in_dim(block, block.shape[dim] - width, None, axis=dim), axis, forward
        )
        high = lax.ppermute(lax.slice_in_dim(block, 0, width, axis=dim), axis, backward)
        block = jnp.concatenate([low, block, high], axis=dim)
    return block


def from_behind(block, axis, distance):
    devices = range(lax.axis_size(axis))
    route = [(i - distance, i) for i in devices if i - distance in devices]
    return lax.ppermute(block, axis, route)


def harmonic(near_value, far_value):
    summed = near_value + far_value
    divisor = jnp.where(summed > 0, summed, 1.0)
    return 2.0 * near_value * far_value / divisor


def neighbours(padded, row_count):
    widened = jnp.pad(padded, ((0, 0), (1, 1)))
    return [
        widened[0:row_count, 1:-1],
        widened[2 : row_count + 2, 1:-1],
        widened[1 : row_count + 1, 0:-2],
        widened[1 : row_count + 1, 2:],
    ]


def prepare(summed_pad, storage, source, pressure_old):
    row_count = storage.shape[0]
    trans_pad = summed_pad[0]
    buoy_pad = summed_pad[1]
    drive_pad = buoyancy_scale * summed_pad[2]
    trans_faces = [
        harmonic(trans_pad[1 : row_count + 1], neighbour)
        for neighbour in neighbours(trans_pad, row_count)
    ]
    buoy_faces = [
        harmonic(buoy_pad[1 : row_count + 1], neighbour)
        for neighbour in neighbours(buoy_pad, row_count)
    ]
    drive_centre = drive_pad[1 : row_count + 1]
    gravity_drive = sum(
        (
            face_coef * (neighbour - drive_centre)
            for face_coef, neighbour in zip(buoy_faces, neighbours(drive_pad, row_count))
        )
    )
    right_hand = storage * pressure_old + source + gravity_drive
    diagonal = storage + trans_faces[0] + trans_faces[1] + trans_faces[2] + trans_faces[3]
    return (trans_faces, right_hand, diagonal)


def relax(trans_faces, right_hand, diagonal, padded):
    row_count = right_hand.shape[0]
    inflow = sum(
        (
            face_coef * neighbour
            for face_coef, neighbour in zip(trans_faces, neighbours(padded, row_count))
        )
    )
    return (right_hand + inflow) / diagonal


def column_depths(every_thick, layer_count, caprock, plume, limit):
    block_count = every_thick.shape[0] // layer_count

    def add_block(block, carry):
        height, above = carry
        first = block * layer_count
        thick_block = lax.dynamic_slice_in_dim(every_thick, first, layer_count, 0)[:, None, None]
        depth = first + lax.broadcasted_iota(jnp.int32, (layer_count, 1, 1), 0)
        gas = (depth >= caprock[None]) & (depth < plume[None])
        height = height + jnp.sum(jnp.where(gas, thick_block, 0.0), axis=0)
        above = above + jnp.sum(jnp.where(gas & (depth < limit), thick_block, 0.0), axis=0)
        return (height, above)

    zeros = jnp.zeros(caprock.shape, jnp.float32)
    return lax.fori_loop(0, block_count, add_block, (zeros, zeros))


def local(permeability, mobility, thickness, caprock, plume, storage, source, pressure_old):
    layer_count = permeability.shape[0]
    layer_index = lax.axis_index("layer")
    layers = layer_index * layer_count + lax.broadcasted_iota(jnp.int32, permeability.shape, 0)
    open_cell = layers >= caprock[None]
    gas_cell = open_cell & (layers < plume[None])
    layer_thick = thickness[:, None, None]
    conduct = jnp.where(open_cell, permeability * mobility * layer_thick, 0.0)
    every_thick = lax.all_gather(thickness, "layer", axis=0, tiled=True)
    limit = layer_index * layer_count
    gas_height, gas_above = column_depths(every_thick, layer_count, caprock, plume, limit)
    column_parts = jnp.stack(
        [jnp.sum(conduct, axis=0), jnp.sum(jnp.where(gas_cell, conduct, 0.0), axis=0)]
    )
    summed = lax.psum(column_parts, "layer")
    summed = jnp.concatenate([summed, gas_height[None]], axis=0)
    padded = padded_2(summed, (("area", 1),), 1)
    trans_faces, right_hand, diagonal = prepare(padded, storage, source, pressure_old)
    pressure = pressure_old
    for sweep_index in range(SWEEPS):
        pressure_pad = padded_2(pressure, (("area", 0),), 1)
        pressure = relax(trans_faces, right_hand, diagonal, pressure_pad)
    layer_mass = layer_thick * jnp.where(gas_cell, gas_density, brine_density)
    depth_all = lax.broadcasted_iota(jnp.int32, every_thick.shape, 0)
    thick_over = jnp.sum(jnp.where(depth_all < limit, every_thick, 0.0))
    mass_over = thick_over - (brine_density - gas_density) * gas_above
    hydro_head = mass_over[None] + jnp.cumsum(layer_mass, axis=0) - 0.5 * layer_mass
    cell_pressure = pressure[None] + gravity_scale * hydro_head
    edge_rows = jnp.stack([conduct[:, 0, :], cell_pressure[:, 0, :]])
    beyond = from_behind(edge_rows, "area", -1)
    next_conduct = jnp.concatenate([conduct[:, 1:, :], beyond[0][:, None, :]], axis=1)
    next_pressure = jnp.concatenate([cell_pressure[:, 1:, :], beyond[1][:, None, :]], axis=1)
    flux_rows = harmonic(conduct, next_conduct) * (cell_pressure - next_pressure)
    side_conduct = jnp.pad(conduct[:, :, 1:], ((0, 0), (0, 0), (0, 1)))
    side_pressure = jnp.pad(cell_pressure[:, :, 1:], ((0, 0), (0, 0), (0, 1)))
    flux_cols = harmonic(conduct, side_conduct) * (cell_pressure - side_pressure)
    return (cell_pressure, flux_rows, flux_cols)


def solution(mesh):
    in_specs = (
        P("layer", "area", None),
        P("layer", "area", None),
        P("layer"),
        P("area", None),
        P("area", None),
        P("area", None),
        P("area", None),
        P("area", None),
    )
    out_specs = (P("layer", "area", None), P("layer", "area", None), P("layer", "area", None))
    return jax.shard_map(local, mesh=mesh, in_specs=in_specs, out_specs=out_specs, check_vma=False)
```

profile of v0, /device:TPU:4, one launch (start us, length us, event | category | flops | bytes accessed | tf_op | source)
XLA Modules:
  0.0 176.6 jit_solution(2895812345910085846)
XLA Ops:
  8.0 1.9 %collective-permute-start.2 = (f32[1,512]{1,0:T(1,128)S(1)}, f32[1,512]{1,0:T(1,128)S(1)}, u32[]{:S(2)}, u32[]{:S(2)}) collective-permute-start(f32[1,512]{1,0:T(1,128)S(1)} %get-tuple-element.191), channel_id=1, source_target_pairs={{0,4},{4,8},{8,12},{12,16},{16,20},{20,24},{24,28},{1,5},{5,9},{9,... | collective-permute-start | bytes 6152 | tf_op jit(solution)/shard_map/ppermute | solution.py:18
  9.9 4.5 %collective-permute-start.3 = (f32[1,512]{1,0:T(1,128)S(1)}, f32[1,512]{1,0:T(1,128)S(1)}, u32[]{:S(2)}, u32[]{:S(2)}) collective-permute-start(f32[1,512]{1,0:T(1,128)S(1)} %get-tuple-element.192), channel_id=1, source_target_pairs={{4,0},{8,4},{12,8},{16,12},{20,16},{24,20},{28,24},{5,1},{9,5},{13... | collective-permute-start | bytes 6152 | tf_op jit(solution)/shard_map/ppermute | solution.py:21
  14.4 7.8 %fusion.59 = (f32[512,512]{1,0:T(8,128)S(1)}, f32[512,512]{1,0:T(8,128)S(1)}, f32[4,512,512]{2,1,0:T(8,128)}) fusion(s32[512,512]{1,0:T(8,128)} %param.14, s32[512,512]{1,0:T(8,128)} %param.13, s32[4]{0:T(128)S(1)} %iota_add_fusion.1, f32[4]{0:T(128)} %param.12, f32[4,512,512]{2,1,0:T(8,128)} %param.10, f32[4,512,512]{2,1,0:T(8,128)} %param.11), kind=kLoop, calls=%fused_computation.138 | loop fusion | flops 8912896 | bytes 16777248 | tf_op jit(solution)/shard_map/reduce_sum | solution.py:113
  22.2 1.5 pad_maximum_fusion.2
  25.2 12.4 %all-reduce.8 = f32[16]{0:T(128)S(1)} all-reduce(f32[16]{0:T(128)S(1)} %dynamic-update-slice), channel_id=1, replica_groups=mesh['area'=8,'layer'=4] {'layer'}, use_global_device_ids=true, to_apply=%add.8 | all-reduce | flops 16 | bytes 128
  37.6 12.6 %while.16 = (s32[]{:T(128)}, f32[512,512]{1,0:T(8,128)S(1)}, f32[512,512]{1,0:T(8,128)}, s32[512,512]{1,0:T(8,128)S(1)}, s32[512,512]{1,0:T(8,128)S(1)}, /*index...) while((s32[]{:T(128)}, f32[512,512]{1,0:T(8,128)S(1)}, ...), condition=%wide.region_6.7_spmd.clone, body=%wide.region_3.0_spmd.clone.sunk | while | flops 8912915 | bytes 18874700 | solution.py:98
  37.7 1.3 select_reduce_fusion.4
  39.8 1.0 copy-done.6
  40.8 1.3 select_reduce_fusion.4
  42.9 1.0 copy-done.6
  44.0 1.3 select_reduce_fusion.4
  46.1 1.0 copy-done.6
  47.1 1.3 select_reduce_fusion.4
  49.2 1.0 copy-done.6
  50.8 59.5 %all-reduce.11.cloned.1.call-done = f32[2,512,512]{2,1,0:T(8,128)} async-done(((f32[2,512,512]{2,1,0:T(8,128)}), f32[2,512,512]{2,1,0:T(8,128)}) %all-reduce.11.cloned.1.call-update) | async-done | bytes 2097168 | tf_op jit(solution)/shard_map/psum | solution.py:115
  111.3 1.9 %collective-permute-start = (f32[3,1,512]{2,1,0:T(1,128)S(1)}, f32[3,1,512]{2,1,0:T(1,128)S(1)}, u32[]{:S(2)}, u32[]{:S(2)}) collective-permute-start(f32[3,1,512]{2,1,0:T(1,128)S(1)} %get-tuple-element.185), channel_id=1, source_target_pairs={{0,4},{4,8},{8,12},{12,16},{16,20},{20,24},{24,28},{1,5},{5,9},{9,... | collective-permute-start | bytes 18440 | tf_op jit(solution)/shard_map/ppermute | solution.py:18
  113.2 4.5 %collective-permute-start.1 = (f32[3,1,512]{2,1,0:T(1,128)S(1)}, f32[3,1,512]{2,1,0:T(1,128)S(1)}, u32[]{:S(2)}, u32[]{:S(2)}) collective-permute-start(f32[3,1,512]{2,1,0:T(1,128)S(1)} %get-tuple-element.186), channel_id=1, source_target_pairs={{4,0},{8,4},{12,8},{16,12},{20,16},{24,20},{28,24},{5,1},{9,5},{13... | collective-permute-start | bytes 18440 | tf_op jit(solution)/shard_map/ppermute | solution.py:21
  117.8 1.6 select_maximum_fusion.4
  121.8 6.4 %fusion.46 = (f32[512,512]{1,0:T(8,128)S(1)}, f32[512,512]{1,0:T(8,128)S(1)}, f32[512,512]{1,0:T(8,128)S(1)}, f32[512,512]{1,0:T(8,128)S(1)}) fusion(f32[514,514]{1,0:T(8,128)S(1)} %select_maximum_fusion.4, f32[1,512]{1,0:T(1,128)S(1)} %collective-permute-done.3, f32[512,512]{1,0:T(8,128)S(1)} %copy-done.9, f32[1,512]{1,0:T(1,128)S(1)} %collective-permute-done.2, ...), kind=kLoop, calls=%fused_computation.98 | loop fusion | flops 20709376 | bytes 21037056 | tf_op jit(solution)/shard_map/div | solution.py:81
  128.2 2.2 %collective-permute-start.4 = (f32[1,512]{1,0:T(1,128)S(1)}, f32[1,512]{1,0:T(1,128)S(1)}, u32[]{:S(2)}, u32[]{:S(2)}) collective-permute-start(f32[1,512]{1,0:T(1,128)S(1)} %get-tuple-element.189), channel_id=1, source_target_pairs={{0,4},{4,8},{8,12},{12,16},{16,20},{20,24},{24,28},{1,5},{5,9},{9,... | collective-permute-start | bytes 6152 | tf_op jit(solution)/shard_map/ppermute | solution.py:18
  130.4 4.3 %collective-permute-start.5 = (f32[1,512]{1,0:T(1,128)S(1)}, f32[1,512]{1,0:T(1,128)S(1)}, u32[]{:S(2)}, u32[]{:S(2)}) collective-permute-start(f32[1,512]{1,0:T(1,128)S(1)} %get-tuple-element.190), channel_id=1, source_target_pairs={{4,0},{8,4},{12,8},{16,12},{20,16},{24,20},{28,24},{5,1},{9,5},{13... | collective-permute-start | bytes 6152 | tf_op jit(solution)/shard_map/ppermute | solution.py:21
  136.4 1.7 fusion.39
  138.2 1.9 %collective-permute-start.6 = (f32[1,512]{1,0:T(1,128)S(1)}, f32[1,512]{1,0:T(1,128)S(1)}, u32[]{:S(2)}, u32[]{:S(2)}) collective-permute-start(f32[1,512]{1,0:T(1,128)S(1)} %get-tuple-element.187), channel_id=1, source_target_pairs={{0,4},{4,8},{8,12},{12,16},{16,20},{20,24},{24,28},{1,5},{5,9},{9,... | collective-permute-start | bytes 6152 | tf_op jit(solution)/shard_map/ppermute | solution.py:18
  140.1 4.7 %collective-permute-start.7 = (f32[1,512]{1,0:T(1,128)S(1)}, f32[1,512]{1,0:T(1,128)S(1)}, u32[]{:S(2)}, u32[]{:S(2)}) collective-permute-start(f32[1,512]{1,0:T(1,128)S(1)} %get-tuple-element.188), channel_id=1, source_target_pairs={{4,0},{8,4},{12,8},{16,12},{20,16},{24,20},{28,24},{5,1},{9,5},{13... | collective-permute-start | bytes 6152 | tf_op jit(solution)/shard_map/ppermute | solution.py:21
  144.8 1.1 collective-permute-done.7
  146.4 1.7 fusion.32
  148.1 2.2 %multiply_add_fusion = f32[4,512,512]{2,1,0:T(8,128)S(1)} fusion(f32[512,512]{1,0:T(8,128)S(1)} %multiply_subtract_fusion, f32[512,512]{1,0:T(8,128)S(1)} %fusion.32, s32[512,512]{1,0:T(8,128)S(1)} %get-tuple-element.281, f32[4]{0:T(128)S(1)} %copy-done.11, s32[512,512]{1,0:T(8,128)S(1)} %get-tuple-element.280, s32[4]{0:T(128)S(1)} %iota_add_fusion.1), kind=kOutput, calls=%fused_computation.17 | output fusion | flops 18874368 | bytes 8388640 | tf_op jit(solution)/shard_map/jit(cumsum)/reduce_window_sum | solution.py:127
  150.3 4.5 %collective-permute-start.8 = (f32[2,4,512]{2,0,1:T(2,128)S(1)}, f32[2,4,512]{2,0,1:T(2,128)S(1)}, u32[]{:S(2)}, u32[]{:S(2)}) collective-permute-start(f32[2,4,512]{2,0,1:T(2,128)S(1)} %pad_maximum_fusion.13), channel_id=1, source_target_pairs={{4,0},{8,4},{12,8},{16,12},{20,16},{24,20},{28,24},{5,1},{9,5},{13... | collective-permute-start | bytes 49160 | tf_op jit(solution)/shard_map/ppermute | solution.py:29
  155.5 1.1 slice.282
  156.6 3.1 %slice.283 = f32[4,512,511]{2,1,0:T(8,128)} slice(f32[4,512,512]{2,1,0:T(8,128)S(1)} %multiply_add_fusion), slice={[0:4], [0:512], [1:512]} | slice | bytes 8372224 | tf_op jit(solution)/shard_map/slice | solution.py:135
  159.7 2.5 %slice.280 = f32[4,511,512]{2,1,0:T(8,128)} slice(f32[4,512,512]{2,1,0:T(8,128)S(1)} %multiply_add_fusion), slice={[0:4], [1:512], [0:512]} | slice | bytes 8372224 | tf_op jit(solution)/shard_map/slice | solution.py:132
  162.3 7.4 %fusion.3 = (f32[4,512,512]{2,1,0:T(8,128)}, f32[4,512,512]{2,1,0:T(8,128)}) fusion(f32[4,512,512]{2,1,0:T(8,128)S(1)} %multiply_add_fusion, f32[4,512,511]{2,1,0:T(8,128)} %slice.283, f32[4,512,512]{2,1,0:T(8,128)S(1)} %copy-done.1, f32[4,512,511]{2,1,0:T(8,128)S(1)} %slice.282, f32[4,1,512]{2,1,0:T(1,128)S(1)} %get-tuple-element.194, ...), kind=kLoop, calls=%fused_computation.14 | loop fusion | flops 17825792 | bytes 33538048 | tf_op jit(solution)/shard_map/mul | solution.py:136
  (81 shorter events, 11.6 us)
Async XLA Ops:
  7.2 103.2 %all-reduce.11.cloned.1.call-start = ((), (), s32[]{:S(2)}) async-start(), calls=%async_computation | async-start | bytes 4194304 | tf_op jit(solution)/shard_map/psum | solution.py:115
  8.0 109.8 %collective-permute-start.2 = (f32[1,512]{1,0:T(1,128)S(1)}, f32[1,512]{1,0:T(1,128)S(1)}, u32[]{:S(2)}, u32[]{:S(2)}) collective-permute-start(f32[1,512]{1,0:T(1,128)S(1)} %get-tuple-element.191), channel_id=1, source_target_pairs={{0,4},{4,8},{8,12},{12,16},{16,20},{20,24},{24,28},{1,5},{5,9},{9,... | collective-permute-start | bytes 6152 | tf_op jit(solution)/shard_map/ppermute | solution.py:18
  9.9 107.9 %collective-permute-start.3 = (f32[1,512]{1,0:T(1,128)S(1)}, f32[1,512]{1,0:T(1,128)S(1)}, u32[]{:S(2)}, u32[]{:S(2)}) collective-permute-start(f32[1,512]{1,0:T(1,128)S(1)} %get-tuple-element.192), channel_id=1, source_target_pairs={{4,0},{8,4},{12,8},{16,12},{20,16},{24,20},{28,24},{5,1},{9,5},{13... | collective-permute-start | bytes 6152 | tf_op jit(solution)/shard_map/ppermute | solution.py:21
  22.2 1.6 copy-start.12
  22.2 2.7 %copy-start.11 = (f32[4]{0:T(128)S(1)}, f32[4]{0:T(128)}, u32[]{:S(2)}) copy-start(f32[4]{0:T(128)} %param.12) | copy-start | bytes 52
  22.2 15.4 %copy-start.2 = (s32[512,512]{1,0:T(8,128)S(1)}, s32[512,512]{1,0:T(8,128)}, u32[]{:S(2)}) copy-start(s32[512,512]{1,0:T(8,128)} %param.13) | copy-start | bytes 3145732
  22.2 15.4 %copy-start.3 = (s32[512,512]{1,0:T(8,128)S(1)}, s32[512,512]{1,0:T(8,128)}, u32[]{:S(2)}) copy-start(s32[512,512]{1,0:T(8,128)} %param.14) | copy-start | bytes 3145732
  37.6 1.4 copy-start.5
  39.8 1.0 copy-start.6
  40.8 1.4 copy-start.5
  42.9 1.0 copy-start.6
  43.9 1.4 copy-start.5
  46.1 1.0 copy-start.6
  47.0 1.4 copy-start.5
  49.2 1.0 copy-start.6
  110.3 9.1 %copy-start.4 = (f32[2,512,512]{2,1,0:T(8,128)S(1)}, f32[2,512,512]{2,1,0:T(8,128)}, u32[]{:S(2)}) copy-start(f32[2,512,512]{2,1,0:T(8,128)} %all-reduce.11.cloned.1.call-done) | copy-start | bytes 6291460
  111.3 8.2 %collective-permute-start = (f32[3,1,512]{2,1,0:T(1,128)S(1)}, f32[3,1,512]{2,1,0:T(1,128)S(1)}, u32[]{:S(2)}, u32[]{:S(2)}) collective-permute-start(f32[3,1,512]{2,1,0:T(1,128)S(1)} %get-tuple-element.185), channel_id=1, source_target_pairs={{0,4},{4,8},{8,12},{12,16},{16,20},{20,24},{24,28},{1,5},{5,9},{9,... | collective-permute-start | bytes 18440 | tf_op jit(solution)/shard_map/ppermute | solution.py:18
  113.2 6.2 %collective-permute-start.1 = (f32[3,1,512]{2,1,0:T(1,128)S(1)}, f32[3,1,512]{2,1,0:T(1,128)S(1)}, u32[]{:S(2)}, u32[]{:S(2)}) collective-permute-start(f32[3,1,512]{2,1,0:T(1,128)S(1)} %get-tuple-element.186), channel_id=1, source_target_pairs={{4,0},{8,4},{12,8},{16,12},{20,16},{24,20},{28,24},{5,1},{9,5},{13... | collective-permute-start | bytes 18440 | tf_op jit(solution)/shard_map/ppermute | solution.py:21
  119.9 1.2 copy-start.8
  119.9 1.5 copy-start.9
  119.9 1.8 %copy-start.10 = (f32[512,512]{1,0:T(8,128)S(1)}, f32[512,512]{1,0:T(8,128)}, u32[]{:S(2)}) copy-start(f32[512,512]{1,0:T(8,128)} %param.16) | copy-start | bytes 3145732
  121.8 12.9 %copy-start.7 = (f32[512,512]{1,0:T(8,128)S(1)}, f32[512,512]{1,0:T(8,128)}, u32[]{:S(2)}) copy-start(f32[512,512]{1,0:T(8,128)} %get-tuple-element.129) | copy-start | bytes 3145732
  128.2 7.2 %collective-permute-start.4 = (f32[1,512]{1,0:T(1,128)S(1)}, f32[1,512]{1,0:T(1,128)S(1)}, u32[]{:S(2)}, u32[]{:S(2)}) collective-permute-start(f32[1,512]{1,0:T(1,128)S(1)} %get-tuple-element.189), channel_id=1, source_target_pairs={{0,4},{4,8},{8,12},{12,16},{16,20},{20,24},{24,28},{1,5},{5,9},{9,... | collective-permute-start | bytes 6152 | tf_op jit(solution)/shard_map/ppermute | solution.py:18
  130.4 5.6 %collective-permute-start.5 = (f32[1,512]{1,0:T(1,128)S(1)}, f32[1,512]{1,0:T(1,128)S(1)}, u32[]{:S(2)}, u32[]{:S(2)}) collective-permute-start(f32[1,512]{1,0:T(1,128)S(1)} %get-tuple-element.190), channel_id=1, source_target_pairs={{4,0},{8,4},{12,8},{16,12},{20,16},{24,20},{28,24},{5,1},{9,5},{13... | collective-permute-start | bytes 6152 | tf_op jit(solution)/shard_map/ppermute | solution.py:21
  136.4 8.4 %copy-start.1 = (f32[4,512,512]{2,1,0:T(8,128)S(1)}, f32[4,512,512]{2,1,0:T(8,128)}, u32[]{:S(2)}) copy-start(f32[4,512,512]{2,1,0:T(8,128)} %get-tuple-element.176) | copy-start | bytes 12582916
  138.2 6.7 %collective-permute-start.6 = (f32[1,512]{1,0:T(1,128)S(1)}, f32[1,512]{1,0:T(1,128)S(1)}, u32[]{:S(2)}, u32[]{:S(2)}) collective-permute-start(f32[1,512]{1,0:T(1,128)S(1)} %get-tuple-element.187), channel_id=1, source_target_pairs={{0,4},{4,8},{8,12},{12,16},{16,20},{20,24},{24,28},{1,5},{5,9},{9,... | collective-permute-start | bytes 6152 | tf_op jit(solution)/shard_map/ppermute | solution.py:18
  140.1 5.8 %collective-permute-start.7 = (f32[1,512]{1,0:T(1,128)S(1)}, f32[1,512]{1,0:T(1,128)S(1)}, u32[]{:S(2)}, u32[]{:S(2)}) collective-permute-start(f32[1,512]{1,0:T(1,128)S(1)} %get-tuple-element.188), channel_id=1, source_target_pairs={{4,0},{8,4},{12,8},{16,12},{20,16},{24,20},{28,24},{5,1},{9,5},{13... | collective-permute-start | bytes 6152 | tf_op jit(solution)/shard_map/ppermute | solution.py:21
  150.3 12.0 %copy-start = (f32[4,512,512]{2,1,0:T(8,128)}, f32[4,512,512]{2,1,0:T(8,128)S(1)}, u32[]{:S(2)}) copy-start(f32[4,512,512]{2,1,0:T(8,128)S(1)} %multiply_add_fusion) | copy-start | bytes 12582916
  150.3 11.9 %collective-permute-start.8 = (f32[2,4,512]{2,0,1:T(2,128)S(1)}, f32[2,4,512]{2,0,1:T(2,128)S(1)}, u32[]{:S(2)}, u32[]{:S(2)}) collective-permute-start(f32[2,4,512]{2,0,1:T(2,128)S(1)} %pad_maximum_fusion.13), channel_id=1, source_target_pairs={{4,0},{8,4},{12,8},{16,12},{20,16},{24,20},{28,24},{5,1},{9,5},{13... | collective-permute-start | bytes 49160 | tf_op jit(solution)/shard_map/ppermute | solution.py:29
Sparse Core Ops, SparseCore 0:
  23.9 86.4 all-reduce.10
where the time goes:
time: 177 us
  waiting for transfers between devices  61.2 us (35%)
  other arithmetic  42.7 us (24%)
  starting transfers between devices  30.6 us (17%)
  between operations  15 us (8%)
  local copies, waits for them, and re-layouts  14.7 us (8%)
  blocking collectives  12.4 us (7%)
    psum x1, waiting for transfers between devices, local(): summed = lax.psum(column_parts, 'layer')  59.5 us
    ppermute x4, starting transfers between devices, padded_2(): lax.ppermute(lax.slice_in_dim(block, 0, width, axis=dim), axis, backward)  18.1 us
    unnamed x1, blocking collectives  12.4 us
    div x3, other arithmetic, relax(): return (right_hand + inflow) / diagonal  9.84 us
    ppermute x4, starting transfers between devices, padded_2(): lax.ppermute(lax.slice_in_dim(block, block.shape[dim] - width, None, axis...  7.92 us
    reduce_sum x1, other arithmetic, local(): jnp.sum(conduct, axis=0)  7.77 us
    mul x1, other arithmetic, local(): harmonic(conduct, side_conduct) * (cell_pressure - side_pressure)  7.44 us
    reduce_sum x4, other arithmetic, add_block(): jnp.sum(jnp.where(gas & (depth < limit), thick_block, 0.0), axis=0)  5.35 us
  transfers between devices with their start and end apart: 10, of which 3 were waited for; matrix products, arithmetic and copies ran while one was open for 17% of the time, Pallas kernels for 0%

commit v1 on v0

--- a/solution.py
+++ b/solution.py
@@ -8,6 +8,11 @@
 gravity_scale = 0.05
 gas_density = 0.7
 brine_density = 1.0
+
+
+def try_all_trees(panel, mesh_dim):
+    upper = jnp.sum(jax.lax.all_gather(panel, mesh_dim), 0)
+    return upper
 
 
 def padded_2(block, sides, width):
@@ -112,7 +117,7 @@
     column_parts = jnp.stack(
         [jnp.sum(conduct, axis=0), jnp.sum(jnp.where(gas_cell, conduct, 0.0), axis=0)]
     )
-    summed = lax.psum(column_parts, "layer")
+    summed = try_all_trees(column_parts, "layer")
     summed = jnp.concatenate([summed, gas_height[None]], axis=0)
     padded = padded_2(summed, (("area", 1),), 1)
     trans_faces, right_hand, diagonal = prepare(padded, storage, source, pressure_old)

time: 177 us -> 236 us (1.33)
  waiting for transfers between devices: 61.2 us -> 118 us
  other arithmetic: 42.7 us -> 45.9 us
    all_gather x0 -> x1, waiting for transfers between devices: none -> 117 us  [try_all_trees(): upper = jnp.sum(jax.lax.all_gather(panel, mesh_dim), 0)]
    psum x1 -> x0, waiting for transfers between devices: 59.5 us -> none  [local(): summed = lax.psum(column_parts, 'layer')]
    reduce_sum x0 -> x1, other arithmetic: none -> 4.65 us  [try_all_trees(): upper = jnp.sum(jax.lax.all_gather(panel, mesh_dim), 0)]
  transfers between devices with their start and end apart: 10 -> 10, of which waited for: 3 -> 3; matrix products, arithmetic and copies ran while one was open for 17% -> 10% of each run, Pallas kernels for 0% -> 0%
where the time goes in v1:
time: 236 us; the launch traced here: 235 us
  waiting for transfers between devices  118 us (50%)
  other arithmetic  45.9 us (19%)
  starting transfers between devices  30.6 us (13%)
  between operations  15.1 us (6%)
  local copies, waits for them, and re-layouts  12.7 us (5%)
  blocking collectives  12.5 us (5%)
    all_gather x1, waiting for transfers between devices, try_all_trees(): upper = jnp.sum(jax.lax.all_gather(panel, mesh_dim), 0)  117 us
    ppermute x4, starting transfers between devices, padded_2(): lax.ppermute(lax.slice_in_dim(block, 0, width, axis=dim), axis, backward)  18.1 us
    unnamed x1, blocking collectives  12.5 us
    div x3, other arithmetic, relax(): return (right_hand + inflow) / diagonal  9.97 us
    ppermute x4, starting transfers between devices, padded_2(): lax.ppermute(lax.slice_in_dim(block, block.shape[dim] - width, None, axis...  7.89 us
    reduce_sum x1, other arithmetic, local(): jnp.sum(conduct, axis=0)  7.77 us
    mul x1, other arithmetic, local(): harmonic(conduct, side_conduct) * (cell_pressure - side_pressure)  6.8 us
    reduce_sum x4, other arithmetic, add_block(): jnp.sum(jnp.where(gas & (depth < limit), thick_block, 0.0), axis=0)  5.35 us
  transfers between devices with their start and end apart: 10, of which 3 were waited for; matrix products, arithmetic and copies ran while one was open for 10% of the time, Pallas kernels for 0%

profile of v1, /device:TPU:4, one launch (start us, length us, event | category | flops | bytes accessed | tf_op | source)
XLA Modules:
  0.0 235.1 jit_solution(4518132792143774374)
XLA Ops:
  7.2 7.8 %fusion.59 = (f32[512,512]{1,0:T(8,128)S(1)}, f32[512,512]{1,0:T(8,128)S(1)}, f32[4,512,512]{2,1,0:T(8,128)}) fusion(s32[512,512]{1,0:T(8,128)} %param.14, s32[512,512]{1,0:T(8,128)} %param.13, s32[4]{0:T(128)S(1)} %iota_add_fusion.1, f32[4]{0:T(128)} %param.12, f32[4,512,512]{2,1,0:T(8,128)} %param.10, f32[4,512,512]{2,1,0:T(8,128)} %param.11), kind=kLoop, calls=%fused_computation.138 | loop fusion | flops 8912896 | bytes 16777248 | tf_op jit(solution)/shard_map/reduce_sum | solution.py:118
  15.0 1.5 pad_maximum_fusion.2
  17.3 1.9 collective-permute-start.2
  19.2 4.5 %collective-permute-start.3 = (f32[1,512]{1,0:T(1,128)S(1)}, f32[1,512]{1,0:T(1,128)S(1)}, u32[]{:S(2)}, u32[]{:S(2)}) collective-permute-start(f32[1,512]{1,0:T(1,128)S(1)} %get-tuple-element.192), channel_id=1, source_target_pairs={{4,0},{8,4},{12,8},{16,12},{20,16},{24,20},{28,24},{5,1},{9,5},{13... | collective-permute-start | bytes 6152 | tf_op jit(solution)/shard_map/ppermute | solution.py:26
  25.3 12.5 %all-reduce.8 = f32[16]{0:T(128)S(1)} all-reduce(f32[16]{0:T(128)S(1)} %dynamic-update-slice), channel_id=1, replica_groups=mesh['area'=8,'layer'=4] {'layer'}, use_global_device_ids=true, to_apply=%add.8 | all-reduce | flops 16 | bytes 128
  38.4 12.6 %while.16 = (s32[]{:T(128)}, f32[512,512]{1,0:T(8,128)S(1)}, f32[512,512]{1,0:T(8,128)}, s32[512,512]{1,0:T(8,128)S(1)}, s32[512,512]{1,0:T(8,128)S(1)}, /*index...) while((s32[]{:T(128)}, f32[512,512]{1,0:T(8,128)S(1)}, ...), condition=%wide.region_6.7_spmd.clone, body=%wide.region_3.0_spmd.clone.sunk | while | flops 8912915 | bytes 18874700 | solution.py:103
  38.5 1.3 select_reduce_fusion.4
  40.6 1.0 copy-done.7
  41.6 1.3 select_reduce_fusion.4
  43.7 1.0 copy-done.7
  44.8 1.3 select_reduce_fusion.4
  46.9 1.0 copy-done.7
  47.9 1.3 select_reduce_fusion.4
  51.0 116.6 %all-gather.3.cloned.1.call-done = f32[8,512,512]{2,1,0:T(8,128)} async-done(((f32[2,512,512]{2,1,0:T(8,128)}), f32[8,512,512]{2,1,0:T(8,128)}) %all-gather.3.cloned.1.call-update) | async-done | bytes 8388624 | tf_op jit(solution)/shard_map/all_gather | solution.py:14
  167.6 4.7 %reduce_sum.64 = f32[2,512,512]{2,1,0:T(8,128)S(1)} reduce(f32[4,2,512,512]{3,2,1,0:T(8,128)} %bitcast.90, f32[]{:T(128)} %constant.56.clone.1), dimensions={0}, to_apply=%region_2.3 | reduce | flops 1572864 | bytes 10485764 | tf_op jit(solution)/shard_map/reduce_sum | solution.py:14
  172.3 1.9 collective-permute-start
  174.2 4.5 %collective-permute-start.1 = (f32[3,1,512]{2,1,0:T(1,128)S(1)}, f32[3,1,512]{2,1,0:T(1,128)S(1)}, u32[]{:S(2)}, u32[]{:S(2)}) collective-permute-start(f32[3,1,512]{2,1,0:T(1,128)S(1)} %get-tuple-element.186), channel_id=1, source_target_pairs={{4,0},{8,4},{12,8},{16,12},{20,16},{24,20},{28,24},{5,1},{9,5},{13... | collective-permute-start | bytes 18440 | tf_op jit(solution)/shard_map/ppermute | solution.py:26
  178.8 1.6 select_maximum_fusion.4
  182.8 6.5 %fusion.46 = (f32[512,512]{1,0:T(8,128)S(1)}, f32[512,512]{1,0:T(8,128)S(1)}, f32[512,512]{1,0:T(8,128)S(1)}, f32[512,512]{1,0:T(8,128)S(1)}) fusion(f32[514,514]{1,0:T(8,128)S(1)} %select_maximum_fusion.4, f32[1,512]{1,0:T(1,128)S(1)} %collective-permute-done.3, f32[512,512]{1,0:T(8,128)S(1)} %copy-done.10, f32[1,512]{1,0:T(1,128)S(1)} %collective-permute-done.2, ...), kind=kLoop, calls=%fused_computation.98 | loop fusion | flops 20709376 | bytes 21037056 | tf_op jit(solution)/shard_map/div | solution.py:86
  189.2 2.1 collective-permute-start.4
  191.4 4.3 %collective-permute-start.5 = (f32[1,512]{1,0:T(1,128)S(1)}, f32[1,512]{1,0:T(1,128)S(1)}, u32[]{:S(2)}, u32[]{:S(2)}) collective-permute-start(f32[1,512]{1,0:T(1,128)S(1)} %get-tuple-element.190), channel_id=1, source_target_pairs={{4,0},{8,4},{12,8},{16,12},{20,16},{24,20},{28,24},{5,1},{9,5},{13... | collective-permute-start | bytes 6152 | tf_op jit(solution)/shard_map/ppermute | solution.py:26
  197.5 1.8 fusion.39
  199.2 1.9 collective-permute-start.6
  201.2 4.7 %collective-permute-start.7 = (f32[1,512]{1,0:T(1,128)S(1)}, f32[1,512]{1,0:T(1,128)S(1)}, u32[]{:S(2)}, u32[]{:S(2)}) collective-permute-start(f32[1,512]{1,0:T(1,128)S(1)} %get-tuple-element.188), channel_id=1, source_target_pairs={{4,0},{8,4},{12,8},{16,12},{20,16},{24,20},{28,24},{5,1},{9,5},{13... | collective-permute-start | bytes 6152 | tf_op jit(solution)/shard_map/ppermute | solution.py:26
  205.9 1.1 collective-permute-done.7
  207.5 1.7 fusion.32
  209.2 2.2 multiply_add_fusion
  211.5 4.5 %collective-permute-start.8 = (f32[2,4,512]{2,0,1:T(2,128)S(1)}, f32[2,4,512]{2,0,1:T(2,128)S(1)}, u32[]{:S(2)}, u32[]{:S(2)}) collective-permute-start(f32[2,4,512]{2,0,1:T(2,128)S(1)} %pad_maximum_fusion.13), channel_id=1, source_target_pairs={{4,0},{8,4},{12,8},{16,12},{20,16},{24,20},{28,24},{5,1},{9,5},{13... | collective-permute-start | bytes 49160 | tf_op jit(solution)/shard_map/ppermute | solution.py:34
  216.7 1.1 slice.282
  217.8 1.1 slice.283
  219.0 2.5 %slice.280 = f32[4,511,512]{2,1,0:T(8,128)} slice(f32[4,512,512]{2,1,0:T(8,128)S(1)} %multiply_add_fusion), slice={[0:4], [1:512], [0:512]} | slice | bytes 8372224 | tf_op jit(solution)/shard_map/slice | solution.py:137
  221.5 6.8 %fusion.3 = (f32[4,512,512]{2,1,0:T(8,128)}, f32[4,512,512]{2,1,0:T(8,128)}) fusion(f32[4,512,512]{2,1,0:T(8,128)S(1)} %multiply_add_fusion, f32[4,512,511]{2,1,0:T(8,128)S(1)} %slice.283, f32[4,512,512]{2,1,0:T(8,128)S(1)} %copy-done.1, f32[4,512,511]{2,1,0:T(8,128)S(1)} %slice.282, f32[4,1,512]{2,1,0:T(1,128)S(1)} %get-tuple-element.194, ...), kind=kLoop, calls=%fused_computation.14 | loop fusion | flops 17825792 | bytes 33538048 | tf_op jit(solution)/shard_map/mul | solution.py:141
  (84 shorter events, 11.6 us)
Async XLA Ops:
  7.2 160.5 %all-gather.3.cloned.1.call-start = ((), (), s32[]{:S(2)}) async-start(), calls=%async_computation | async-start | bytes 10485760 | tf_op jit(solution)/shard_map/all_gather | solution.py:14
  15.0 8.8 %copy-start.13 = (u32[32]{0:T(128)S(1)}, u32[32]{0:T(128)}, u32[]{:S(2)}) copy-start(u32[32]{0:T(128)} %constant.82) | copy-start | bytes 388
  15.0 10.0 %copy-start.12 = (f32[4]{0:T(128)S(1)}, f32[4]{0:T(128)}, u32[]{:S(2)}) copy-start(f32[4]{0:T(128)} %param.12) | copy-start | bytes 52
  15.0 23.4 %copy-start.2 = (s32[512,512]{1,0:T(8,128)S(1)}, s32[512,512]{1,0:T(8,128)}, u32[]{:S(2)}) copy-start(s32[512,512]{1,0:T(8,128)} %param.13) | copy-start | bytes 3145732
  15.0 23.4 %copy-start.4 = (s32[512,512]{1,0:T(8,128)S(1)}, s32[512,512]{1,0:T(8,128)}, u32[]{:S(2)}) copy-start(s32[512,512]{1,0:T(8,128)} %param.14) | copy-start | bytes 3145732
  17.3 161.5 %collective-permute-start.2 = (f32[1,512]{1,0:T(1,128)S(1)}, f32[1,512]{1,0:T(1,128)S(1)}, u32[]{:S(2)}, u32[]{:S(2)}) collective-permute-start(f32[1,512]{1,0:T(1,128)S(1)} %get-tuple-element.191), channel_id=1, source_target_pairs={{0,4},{4,8},{8,12},{12,16},{16,20},{20,24},{24,28},{1,5},{5,9},{9,... | collective-permute-start | bytes 6152 | tf_op jit(solution)/shard_map/ppermute | solution.py:23
  19.2 159.6 %collective-permute-start.3 = (f32[1,512]{1,0:T(1,128)S(1)}, f32[1,512]{1,0:T(1,128)S(1)}, u32[]{:S(2)}, u32[]{:S(2)}) collective-permute-start(f32[1,512]{1,0:T(1,128)S(1)} %get-tuple-element.192), channel_id=1, source_target_pairs={{4,0},{8,4},{12,8},{16,12},{20,16},{24,20},{28,24},{5,1},{9,5},{13... | collective-permute-start | bytes 6152 | tf_op jit(solution)/shard_map/ppermute | solution.py:26
  38.4 1.4 copy-start.6
  40.6 1.0 copy-start.7
  41.5 1.4 copy-start.6
  43.7 1.0 copy-start.7
  44.7 1.4 copy-start.6
  46.9 1.0 copy-start.7
  47.8 1.4 copy-start.6
  50.0 1.0 copy-start.7
  172.3 8.2 %collective-permute-start = (f32[3,1,512]{2,1,0:T(1,128)S(1)}, f32[3,1,512]{2,1,0:T(1,128)S(1)}, u32[]{:S(2)}, u32[]{:S(2)}) collective-permute-start(f32[3,1,512]{2,1,0:T(1,128)S(1)} %get-tuple-element.185), channel_id=1, source_target_pairs={{0,4},{4,8},{8,12},{12,16},{16,20},{20,24},{24,28},{1,5},{5,9},{9,... | collective-permute-start | bytes 18440 | tf_op jit(solution)/shard_map/ppermute | solution.py:23
  174.2 6.2 %collective-permute-start.1 = (f32[3,1,512]{2,1,0:T(1,128)S(1)}, f32[3,1,512]{2,1,0:T(1,128)S(1)}, u32[]{:S(2)}, u32[]{:S(2)}) collective-permute-start(f32[3,1,512]{2,1,0:T(1,128)S(1)} %get-tuple-element.186), channel_id=1, source_target_pairs={{4,0},{8,4},{12,8},{16,12},{20,16},{24,20},{28,24},{5,1},{9,5},{13... | collective-permute-start | bytes 18440 | tf_op jit(solution)/shard_map/ppermute | solution.py:26
  180.9 1.2 copy-start.9
  180.9 1.5 copy-start.10
  180.9 1.8 copy-start.11
  182.8 13.0 %copy-start.8 = (f32[512,512]{1,0:T(8,128)S(1)}, f32[512,512]{1,0:T(8,128)}, u32[]{:S(2)}) copy-start(f32[512,512]{1,0:T(8,128)} %get-tuple-element.129) | copy-start | bytes 3145732
  189.2 7.2 %collective-permute-start.4 = (f32[1,512]{1,0:T(1,128)S(1)}, f32[1,512]{1,0:T(1,128)S(1)}, u32[]{:S(2)}, u32[]{:S(2)}) collective-permute-start(f32[1,512]{1,0:T(1,128)S(1)} %get-tuple-element.189), channel_id=1, source_target_pairs={{0,4},{4,8},{8,12},{12,16},{16,20},{20,24},{24,28},{1,5},{5,9},{9,... | collective-permute-start | bytes 6152 | tf_op jit(solution)/shard_map/ppermute | solution.py:23
  191.4 5.6 %collective-permute-start.5 = (f32[1,512]{1,0:T(1,128)S(1)}, f32[1,512]{1,0:T(1,128)S(1)}, u32[]{:S(2)}, u32[]{:S(2)}) collective-permute-start(f32[1,512]{1,0:T(1,128)S(1)} %get-tuple-element.190), channel_id=1, source_target_pairs={{4,0},{8,4},{12,8},{16,12},{20,16},{24,20},{28,24},{5,1},{9,5},{13... | collective-permute-start | bytes 6152 | tf_op jit(solution)/shard_map/ppermute | solution.py:26
  197.4 8.4 %copy-start.1 = (f32[4,512,512]{2,1,0:T(8,128)S(1)}, f32[4,512,512]{2,1,0:T(8,128)}, u32[]{:S(2)}) copy-start(f32[4,512,512]{2,1,0:T(8,128)} %get-tuple-element.176) | copy-start | bytes 12582916
  199.2 6.7 %collective-permute-start.6 = (f32[1,512]{1,0:T(1,128)S(1)}, f32[1,512]{1,0:T(1,128)S(1)}, u32[]{:S(2)}, u32[]{:S(2)}) collective-permute-start(f32[1,512]{1,0:T(1,128)S(1)} %get-tuple-element.187), channel_id=1, source_target_pairs={{0,4},{4,8},{8,12},{12,16},{16,20},{20,24},{24,28},{1,5},{5,9},{9,... | collective-permute-start | bytes 6152 | tf_op jit(solution)/shard_map/ppermute | solution.py:23
  201.2 5.8 %collective-permute-start.7 = (f32[1,512]{1,0:T(1,128)S(1)}, f32[1,512]{1,0:T(1,128)S(1)}, u32[]{:S(2)}, u32[]{:S(2)}) collective-permute-start(f32[1,512]{1,0:T(1,128)S(1)} %get-tuple-element.188), channel_id=1, source_target_pairs={{4,0},{8,4},{12,8},{16,12},{20,16},{24,20},{28,24},{5,1},{9,5},{13... | collective-permute-start | bytes 6152 | tf_op jit(solution)/shard_map/ppermute | solution.py:26
  207.5 1.8 copy-start.3
  207.5 1.8 copy-start.5
  211.4 10.0 %copy-start = (f32[4,512,512]{2,1,0:T(8,128)}, f32[4,512,512]{2,1,0:T(8,128)S(1)}, u32[]{:S(2)}) copy-start(f32[4,512,512]{2,1,0:T(8,128)S(1)} %multiply_add_fusion) | copy-start | bytes 12582916
  211.5 10.0 %collective-permute-start.8 = (f32[2,4,512]{2,0,1:T(2,128)S(1)}, f32[2,4,512]{2,0,1:T(2,128)S(1)}, u32[]{:S(2)}, u32[]{:S(2)}) collective-permute-start(f32[2,4,512]{2,0,1:T(2,128)S(1)} %pad_maximum_fusion.13), channel_id=1, source_target_pairs={{4,0},{8,4},{12,8},{16,12},{20,16},{24,20},{28,24},{5,1},{9,5},{13... | collective-permute-start | bytes 49160 | tf_op jit(solution)/shard_map/ppermute | solution.py:34
Sparse Core Ops, SparseCore 0:
  16.6 150.9 all-gather.2
